TPU v7x, 512 devices: a whole 4x8x8 slice. The times are simulated.
512 devices in a mesh: section: 16 (over y, core), expert: 32 (over x, z).
Axes of the slice: x: 4, y: 8, z: 8, core: 2. Of those that a mesh axis runs over, the one named last changes fastest.
Arguments:
- tokens: bfloat16 [16, 2048, 2560], P('section', 'expert'), may hold values from -6 to 6
- norm_gain: float32 [16, 2560], P('section'), may hold values from 0.25 to 1.75
- w_gate: bfloat16 [16, 32, 2560, 192], P('section', 'expert'), may hold values from -0.125 to 0.125
- w_up: bfloat16 [16, 32, 2560, 192], P('section', 'expert'), may hold values from -0.125 to 0.125
- w_down: bfloat16 [16, 32, 192, 2560], P('section', 'expert'), may hold values from -0.21875 to 0.21875
- routes: int32 [16, 2, 2048, 1], P('section', None, 'expert'), may hold values from 0 to 7; in each aligned block of 64 rows (0 to 63, 64 to 127, ..., all dimensions but the last counted through in order) at most 9 rows name the same one
- mix_weights: float32 [16, 2, 2048, 1], P('section', None, 'expert'), may hold values from 0.1 to 1
- cotangent: bfloat16 [16, 2048, 2560], P('section', 'expert'), may hold values from -6 to 6
Outputs:
- final: bfloat16 [16, 2048, 2560], P('section', 'expert')
- input_grads: bfloat16 [16, 2048, 2560], P('section', 'expert')
Inputs may be any that keep to these rules, and one draw needn't show every extreme that they name: `routes`: the 1 ids of a token differ. In the rows of one device (aligned blocks of 64 tokens of one layer and step) no id is named by more than 9 tokens, a bound that some block reaches.
All inputs are finite; a program needn't handle non-finite values.
Results may differ from a plain program's by a relative error of at most 0.011.
Values may be sent and summed in bfloat16 or wider, within the bound.
A program may use at most 64 MiB of HBM per device.

v0:
```python
import jax
import jax.numpy as jnp
from jax import lax
from jax.sharding import PartitionSpec as P

SPLIT = 4


EPSILON = 1e-06


def from_behind(value, axis, steps):
    count = lax.axis_size(axis)
    pairs = [(source, (source + steps) % count) for source in range(count)]
    return lax.ppermute(value, axis, pairs)


def norm_apply(hidden_f, gain_row):
    inv_scale = lax.rsqrt(jnp.mean(hidden_f * hidden_f, axis=-1, keepdims=True) + EPSILON)
    return hidden_f * inv_scale * gain_row


def slot_index(route_ids, experts, capacity):
    labels = jnp.arange(experts, dtype=jnp.int32)
    chosen = jnp.sum((route_ids[:, :, None] == labels[None, None, :]).astype(jnp.int32), axis=1)
    before = jnp.cumsum(chosen, axis=0) - chosen
    within = jnp.take_along_axis(before, route_ids, axis=1)
    return route_ids * capacity + within


def local(tokens, norm_gain, w_gate, w_up, w_down, routes, mix_weights, cotangent):
    owners = lax.axis_size("expert")
    experts = owners // SPLIT
    tok_rows = tokens.shape[1]
    model_width = tokens.shape[2]
    top_count = routes.shape[3]
    steps_count = routes.shape[1]
    capacity = tok_rows * top_count // experts + max(1, tok_rows * top_count // (16 * experts))
    slot_total = experts * capacity
    gain_row = norm_gain[0]
    gate_w = w_gate[0, 0]
    up_w = w_up[0, 0]
    down_w = w_down[0, 0]

    def make_boxes(select, values):
        return jnp.dot(select, values, preferred_element_type=jnp.float32).astype(jnp.bfloat16)

    def every_slice(boxes):
        return jnp.repeat(boxes.reshape(experts, capacity, model_width), SPLIT, axis=0)

    def add_slices(returned):
        summed = jnp.sum(
            returned.reshape(experts, SPLIT, capacity, model_width).astype(jnp.float32), axis=1
        )
        return summed.astype(jnp.bfloat16).reshape(slot_total, model_width)

    hidden = tokens[0]
    stored = []
    for step_index in range(steps_count):
        slot_ids = slot_index(routes[0, step_index], experts, capacity)
        positions = lax.broadcasted_iota(jnp.int32, (slot_total, tok_rows, top_count), 0)
        select = jnp.sum((positions == slot_ids[None]).astype(jnp.float32), axis=2).astype(
            jnp.bfloat16
        )
        boxes = make_boxes(
            select, norm_apply(hidden.astype(jnp.float32), gain_row).astype(jnp.bfloat16)
        )
        slot_rows = lax.all_to_all(
            every_slice(boxes), "expert", split_axis=0, concat_axis=0, tiled=True
        )
        expert_gate_act = jnp.einsum(
            "ncd,dh->nch", slot_rows, gate_w, preferred_element_type=jnp.float32
        )
        expert_upper = jnp.einsum(
            "ncd,dh->nch", slot_rows, up_w, preferred_element_type=jnp.float32
        )
        inner_act = (jax.nn.silu(expert_gate_act) * expert_upper).astype(jnp.bfloat16)
        outputs = jnp.einsum("nch,hd->ncd", inner_act, down_w, preferred_element_type=jnp.float32)
        outputs, received, gate_kept, upper_kept = (
            outputs.astype(jnp.bfloat16),
            slot_rows,
            expert_gate_act,
            expert_upper,
        )
        returned = add_slices(
            lax.all_to_all(outputs, "expert", split_axis=0, concat_axis=0, tiled=True)
        )
        picked = returned[slot_ids].astype(jnp.float32)
        combined = jnp.sum(mix_weights[0, step_index][:, :, None] * picked, axis=1)
        stored.append((hidden, slot_ids, select, received, gate_kept, upper_kept))
        hidden = (hidden.astype(jnp.float32) + combined).astype(jnp.bfloat16)
        if step_index + 1 < steps_count:
            hidden = from_behind(hidden, "section", 1)
    grad_now = cotangent[0]
    for step_index in reversed(range(steps_count)):
        start_hidden, slot_ids, select, received, gate_kept, upper_kept = stored[step_index]
        grad_boxes = make_boxes(select, grad_now)
        grads_in = lax.all_to_all(
            every_slice(grad_boxes), "expert", split_axis=0, concat_axis=0, tiled=True
        )
        sigmoid_gate = jax.nn.sigmoid(gate_kept)
        d_inner = jnp.einsum("ncd,hd->nch", grads_in, down_w, preferred_element_type=jnp.float32)
        d_gate = (
            d_inner * upper_kept * sigmoid_gate * (1.0 + gate_kept * (1.0 - sigmoid_gate))
        ).astype(jnp.bfloat16)
        d_upper = (d_inner * gate_kept * sigmoid_gate).astype(jnp.bfloat16)
        part_rows = jnp.einsum("nch,dh->ncd", d_gate, gate_w, preferred_element_type=jnp.float32)
        part_rows = part_rows + jnp.einsum(
            "nch,dh->ncd", d_upper, up_w, preferred_element_type=jnp.float32
        )
        returned = add_slices(
            lax.all_to_all(
                part_rows.astype(jnp.bfloat16), "expert", split_axis=0, concat_axis=0, tiled=True
            )
        )
        picked = returned[slot_ids].astype(jnp.float32)
        d_normed = jnp.sum(mix_weights[0, step_index][:, :, None] * picked, axis=1)
        _, pullback = jax.vjp(
            lambda values: norm_apply(values, gain_row), start_hidden.astype(jnp.float32)
        )
        grad_now = (grad_now.astype(jnp.float32) + pullback(d_normed)[0]).astype(jnp.bfloat16)
        if step_index > 0:
            grad_now = from_behind(grad_now, "section", -1)
    return (hidden[None], grad_now[None])


def solution(mesh):
    in_specs = (
        P("section", "expert", None),
        P("section", None),
        P("section", "expert", None, None),
        P("section", "expert", None, None),
        P("section", "expert", None, None),
        P("section", None, "expert", None),
        P("section", None, "expert", None),
        P("section", "expert", None),
    )
    out_specs = (P("section", "expert", None), P("section", "expert", None))
    return jax.shard_map(local, mesh=mesh, in_specs=in_specs, out_specs=out_specs, check_vma=False)
```

profile of v0, /device:TPU:88, one launch (start us, length us, event | category | flops | bytes accessed | tf_op | source)
XLA Modules:
  0.0 608.1 jit_solution(2136870238932072688)
XLA Ops:
  9.2 75.1 %all_to_all.40 = bf16[32,9,2560]{2,1,0:T(8,128)(2,1)S(1)} all-to-all(bf16[32,9,2560]{2,1,0:T(8,128)(2,1)S(1)} %bitcast.141), channel_id=1, replica_groups=mesh['section'=16,'expert'=32] {'expert'}, dimensions={0} | all-to-all | bytes 2949120 | tf_op jit(solution)/shard_map/all_to_all | solution.py:68
  88.0 2.4 copy.20
  90.4 5.0 all-to-all-start.1
  95.5 60.2 %all-to-all-done.1 = bf16[32,9,2560]{2,1,0:T(8,128)(2,1)} async-done(((bf16[32,9,2560]{2,1,0:T(8,128)(2,1)}), bf16[32,9,2560]{2,1,0:T(8,128)(2,1)}, u32[]{:S(2)}, u32[]{:S(2)}) %all-to-all-start.1) | async-done | bytes 1474592 | tf_op jit(solution)/shard_map/all_to_all | solution.py:86
  155.7 3.2 bitcast_reduce_fusion.3
  161.2 6.5 %collective-permute-done = bf16[64,2560]{1,0:T(8,128)(2,1)S(1)} collective-permute-done((bf16[64,2560]{1,0:T(8,128)(2,1)S(1)}, bf16[64,2560]{1,0:T(8,128)(2,1)S(1)}, u32[]{:S(2)}, u32[]{:S(2)}) %collective-permute-start) | collective-permute-done | bytes 327712 | tf_op jit(solution)/shard_map/ppermute | solution.py:15
  171.9 7.8 %all-to-all-start.2 = ((bf16[32,9,2560]{2,1,0:T(8,128)(2,1)}), bf16[32,9,2560]{2,1,0:T(8,128)(2,1)}, u32[]{:S(2)}, u32[]{:S(2)}) async-start(bf16[32,9,2560]{2,1,0:T(8,128)(2,1)} %bitcast.140), calls=%async_computation.2 | async-start | bytes 5242880 | tf_op jit(solution)/shard_map/all_to_all | solution.py:68
  181.9 59.8 %all-to-all-done.2 = bf16[32,9,2560]{2,1,0:T(8,128)(2,1)} async-done(((bf16[32,9,2560]{2,1,0:T(8,128)(2,1)}), bf16[32,9,2560]{2,1,0:T(8,128)(2,1)}, u32[]{:S(2)}, u32[]{:S(2)}) %all-to-all-start.2) | async-done | bytes 1474592 | tf_op jit(solution)/shard_map/all_to_all | solution.py:68
  243.6 7.7 %all-to-all-start.4 = ((bf16[32,9,2560]{2,1,0:T(8,128)(2,1)}), bf16[32,9,2560]{2,1,0:T(8,128)(2,1)}, u32[]{:S(2)}, u32[]{:S(2)}) async-start(bf16[32,9,2560]{2,1,0:T(8,128)(2,1)} %bitcast.139), calls=%async_computation.4 | async-start | bytes 5242880 | tf_op jit(solution)/shard_map/all_to_all | solution.py:98
  251.3 3.0 fusion.20
  254.2 2.9 fusion.12
  257.7 2.5 copy.25
  260.2 51.7 %all-to-all-done.4 = bf16[32,9,2560]{2,1,0:T(8,128)(2,1)} async-done(((bf16[32,9,2560]{2,1,0:T(8,128)(2,1)}), bf16[32,9,2560]{2,1,0:T(8,128)(2,1)}, u32[]{:S(2)}, u32[]{:S(2)}) %all-to-all-start.4) | async-done | bytes 1474592 | tf_op jit(solution)/shard_map/all_to_all | solution.py:98
  311.9 7.7 %all-to-all-start.3 = ((bf16[32,9,2560]{2,1,0:T(8,128)(2,1)}), bf16[32,9,2560]{2,1,0:T(8,128)(2,1)}, u32[]{:S(2)}, u32[]{:S(2)}) async-start(bf16[32,9,2560]{2,1,0:T(8,128)(2,1)} %copy.25), calls=%async_computation.3 | async-start | bytes 5242880 | tf_op jit(solution)/shard_map/all_to_all | solution.py:86
  319.6 2.9 fusion.4
  324.3 2.4 copy.29
  326.7 53.1 %all-to-all-done.3 = bf16[32,9,2560]{2,1,0:T(8,128)(2,1)} async-done(((bf16[32,9,2560]{2,1,0:T(8,128)(2,1)}), bf16[32,9,2560]{2,1,0:T(8,128)(2,1)}, u32[]{:S(2)}, u32[]{:S(2)}) %all-to-all-start.3) | async-done | bytes 1474592 | tf_op jit(solution)/shard_map/all_to_all | solution.py:86
  379.7 7.7 %all-to-all-start.5 = ((bf16[32,9,2560]{2,1,0:T(8,128)(2,1)}), bf16[32,9,2560]{2,1,0:T(8,128)(2,1)}, u32[]{:S(2)}, u32[]{:S(2)}) async-start(bf16[32,9,2560]{2,1,0:T(8,128)(2,1)} %copy.29), calls=%async_computation.5 | async-start | bytes 5242880 | tf_op jit(solution)/shard_map/all_to_all | solution.py:112
  387.5 3.3 bitcast_reduce_fusion.2
  392.0 55.3 %all-to-all-done.5 = bf16[32,9,2560]{2,1,0:T(8,128)(2,1)} async-done(((bf16[32,9,2560]{2,1,0:T(8,128)(2,1)}), bf16[32,9,2560]{2,1,0:T(8,128)(2,1)}, u32[]{:S(2)}, u32[]{:S(2)}) %all-to-all-start.5) | async-done | bytes 1474592 | tf_op jit(solution)/shard_map/all_to_all | solution.py:112
  447.4 3.2 bitcast_reduce_fusion.1
  456.7 4.6 collective-permute-done.1
  463.7 69.7 %all_to_all.41 = bf16[32,9,2560]{2,1,0:T(8,128)(2,1)S(1)} all-to-all(bf16[32,9,2560]{2,1,0:T(8,128)(2,1)S(1)} %bitcast.142), channel_id=1, replica_groups=mesh['section'=16,'expert'=32] {'expert'}, dimensions={0} | all-to-all | bytes 2949120 | tf_op jit(solution)/shard_map/all_to_all | solution.py:98
  537.3 67.9 %all_to_all.42 = bf16[32,9,2560]{2,1,0:T(8,128)(2,1)S(1)} all-to-all(bf16[32,9,2560]{2,1,0:T(8,128)(2,1)S(1)} %copy.33), channel_id=1, replica_groups=mesh['section'=16,'expert'=32] {'expert'}, dimensions={0} | all-to-all | bytes 2949120 | tf_op jit(solution)/shard_map/all_to_all | solution.py:112
  (94 shorter events, 41.4 us)
Async XLA Ops:
  0.6 86.8 %copy-start = (bf16[1,1,192,2560]{3,2,1,0:T(8,128)(2,1)S(1)}, bf16[1,1,192,2560]{3,2,1,0:T(8,128)(2,1)}, u32[]{:S(2)}) copy-start(bf16[1,1,192,2560]{3,2,1,0:T(8,128)(2,1)} %param.14) | copy-start | bytes 2949124
  9.2 75.1 %copy-start.2 = (bf16[1,1,2560,192]{2,3,1,0:T(8,128)(2,1)S(1)}, bf16[1,1,2560,192]{2,3,1,0:T(8,128)(2,1)}, u32[]{:S(2)}) copy-start(bf16[1,1,2560,192]{2,3,1,0:T(8,128)(2,1)} %param.12) | copy-start | bytes 2949124
  84.3 1.2 copy-start.3
  85.5 1.1 copy-start.7
  86.7 0.7 copy-start.12
  90.4 5.1 copy-start.14
  90.4 65.3 %all-to-all-start.1 = ((bf16[32,9,2560]{2,1,0:T(8,128)(2,1)}), bf16[32,9,2560]{2,1,0:T(8,128)(2,1)}, u32[]{:S(2)}, u32[]{:S(2)}) async-start(bf16[32,9,2560]{2,1,0:T(8,128)(2,1)} %copy.20), calls=%async_computation.1 | async-start | bytes 5242880 | tf_op jit(solution)/shard_map/all_to_all | solution.py:86
  158.9 2.1 copy-start.1
  161.1 6.5 %collective-permute-start = (bf16[64,2560]{1,0:T(8,128)(2,1)S(1)}, bf16[64,2560]{1,0:T(8,128)(2,1)S(1)}, u32[]{:S(2)}, u32[]{:S(2)}) collective-permute-start(bf16[64,2560]{1,0:T(8,128)(2,1)S(1)} %fusion.33), channel_id=1, source_target_pairs={{0,32},{32,64},{64,96},{96,128},{128,160},{160,192},{192,224},{224... | collective-permute-start | bytes 983048 | tf_op jit(solution)/shard_map/ppermute | solution.py:15
  171.9 7.8 %copy-start.9 = (bf16[1,64,2560]{2,1,0:T(8,128)(2,1)S(1)}, bf16[1,64,2560]{2,1,0:T(8,128)(2,1)}, u32[]{:S(2)}) copy-start(bf16[1,64,2560]{2,1,0:T(8,128)(2,1)} %param.17) | copy-start | bytes 983044
  171.9 69.9 %all-to-all-start.2 = ((bf16[32,9,2560]{2,1,0:T(8,128)(2,1)}), bf16[32,9,2560]{2,1,0:T(8,128)(2,1)}, u32[]{:S(2)}, u32[]{:S(2)}) async-start(bf16[32,9,2560]{2,1,0:T(8,128)(2,1)} %bitcast.140), calls=%async_computation.2 | async-start | bytes 5242880 | tf_op jit(solution)/shard_map/all_to_all | solution.py:68
  243.6 68.3 %all-to-all-start.4 = ((bf16[32,9,2560]{2,1,0:T(8,128)(2,1)}), bf16[32,9,2560]{2,1,0:T(8,128)(2,1)}, u32[]{:S(2)}, u32[]{:S(2)}) async-start(bf16[32,9,2560]{2,1,0:T(8,128)(2,1)} %bitcast.139), calls=%async_computation.4 | async-start | bytes 5242880 | tf_op jit(solution)/shard_map/all_to_all | solution.py:98
  251.2 3.0 copy-start.4
  311.9 67.9 %all-to-all-start.3 = ((bf16[32,9,2560]{2,1,0:T(8,128)(2,1)}), bf16[32,9,2560]{2,1,0:T(8,128)(2,1)}, u32[]{:S(2)}, u32[]{:S(2)}) async-start(bf16[32,9,2560]{2,1,0:T(8,128)(2,1)} %copy.25), calls=%async_computation.3 | async-start | bytes 5242880 | tf_op jit(solution)/shard_map/all_to_all | solution.py:86
  322.5 1.2 copy-start.5
  379.7 67.6 %all-to-all-start.5 = ((bf16[32,9,2560]{2,1,0:T(8,128)(2,1)}), bf16[32,9,2560]{2,1,0:T(8,128)(2,1)}, u32[]{:S(2)}, u32[]{:S(2)}) async-start(bf16[32,9,2560]{2,1,0:T(8,128)(2,1)} %copy.29), calls=%async_computation.5 | async-start | bytes 5242880 | tf_op jit(solution)/shard_map/all_to_all | solution.py:112
  456.7 4.6 collective-permute-start.1
  461.3 2.4 copy-start.10
  533.4 1.2 copy-start.8
  533.4 1.2 copy-start.13
  534.6 1.2 copy-start.6
  605.7 1.3 copy-start.11
where the time goes:
time: 609 us; the launch traced here: 608 us
  waiting for transfers between devices  291 us (48%)
  blocking collectives  213 us (35%)
  starting transfers between devices  35.9 us (6%)
  local copies, waits for them, and re-layouts  28.1 us (5%)
  matrix products  20.1 us (3%)
  other arithmetic  19 us (3%)
    all_to_all x2, waiting for transfers between devices, local(): lax.all_to_all(outputs, 'expert', split_axis=0, concat_axis=0, tiled=True)  113 us
    all_to_all x1, blocking collectives, local(): lax.all_to_all(every_slice(boxes), 'expert', split_axis=0, concat_axis=0,...  75.1 us
    all_to_all x1, blocking collectives, local(): lax.all_to_all(every_slice(grad_boxes), 'expert', split_axis=0, concat_ax...  69.7 us
    all_to_all x1, blocking collectives, local(): lax.all_to_all(part_rows.astype(jnp.bfloat16), 'expert', split_axis=0, co...  67.9 us
    all_to_all x1, waiting for transfers between devices, local(): lax.all_to_all(every_slice(boxes), 'expert', split_axis=0, concat_axis=0,...  59.8 us
    all_to_all x1, waiting for transfers between devices, local(): lax.all_to_all(part_rows.astype(jnp.bfloat16), 'expert', split_axis=0, co...  55.3 us
    all_to_all x1, waiting for transfers between devices, local(): lax.all_to_all(every_slice(grad_boxes), 'expert', split_axis=0, concat_ax...  51.7 us
    all_to_all x2, starting transfers between devices, local(): lax.all_to_all(outputs, 'expert', split_axis=0, concat_axis=0, tiled=True)  12.7 us
  transfers between devices with their start and end apart: 7, of which 7 were waited for; matrix products, arithmetic and copies ran while one was open for 4% of the time, Pallas kernels for 0%

commit v1 on v0

v1 whole, which is shorter than its diff:
```python
import jax
import jax.numpy as jnp
from jax import lax
from jax.experimental import pallas as pl
from jax.experimental.pallas import tpu as pltpu
from jax.sharding import PartitionSpec as P

MESH = pl.DeviceIdType.MESH
EPSILON = 1e-06
F32 = jnp.float32
BF16 = jnp.bfloat16
XS = 4
ZS = 8
NB = 16
ROWS = 8
LANES = 128


def kernel(
    tokens, gain, wgu, wdn, routes, mix, cotangent, final, grads,
    wgu_other, wd_pair, sends, recvs, back_sends, back_recvs, fold, x_all, gates, uppers, hidden1,
    hop_out, hop_in, d_own, d_other, inner,
    send_sems, recv_sems, bsend_sems, brecv_sems, w_send, w_recv, hop_send, hop_recv,
):
    width = tokens.shape[1]
    toks = tokens.shape[0]
    chunks = width // LANES
    folds = -(-chunks // 8)
    half = 64
    section = lax.axis_index("section")
    sections = lax.axis_size("section")
    me = lax.axis_index("expert")
    x = me // ZS
    z = me % ZS
    sign = 1 - 2 * (z % 2)
    own_half = z // 4
    twist = ((z + 1) // 2) % 2

    def at(xd, zd):
        return {"expert": ((xd + XS) % XS) * ZS + (zd + 2 * ZS) % ZS}

    def target(i):
        j = i % 4
        off = 2 * (j % 2) - 3 * (j // 2)
        return x + i // 4, (z + off * sign + ZS) % ZS

    def origin(i):
        j = i % 4
        off = (2 * (j % 2) - 3 * (j // 2)) * (2 * (j // 2) - 1)
        return x - i // 4, (z + off * sign + ZS) % ZS

    partner = at(x, z + sign)
    after = {"section": (section + 1) % sections}
    before = {"section": (section + sections - 1) % sections}

    barrier = pltpu.get_barrier_semaphore()

    def greet_targets(i, carry):
        xd, zd = target(i)
        pl.semaphore_signal(barrier, inc=1, device_id=at(xd, zd), device_id_type=MESH)
        return carry

    def greet_origins(i, carry):
        xd, zd = origin(i)
        pl.semaphore_signal(barrier, inc=1, device_id=at(xd, zd), device_id_type=MESH)
        return carry

    lax.fori_loop(1, NB, greet_targets, 0)
    lax.fori_loop(1, NB, greet_origins, 0)
    for neighbour in (partner, after, before):
        pl.semaphore_signal(barrier, inc=1, device_id=neighbour, device_id_type=MESH)

    def dispatch_copy(ex, i):
        xd, zd = target(i)
        block = (i // 4) * 2 + (zd // 4 + own_half) % 2
        return pltpu.make_async_remote_copy(
            src_ref=sends.at[ex, pl.ds(pl.multiple_of(block * ROWS, ROWS), ROWS), :],
            dst_ref=recvs.at[ex, pl.ds(pl.multiple_of(i * ROWS, ROWS), ROWS), :],
            send_sem=send_sems.at[ex, i],
            recv_sem=recv_sems.at[ex, i],
            device_id=at(xd, zd),
            device_id_type=MESH,
        )

    def back_copy(ex, i):
        xd, zd = origin(i)
        rows = pl.ds(pl.multiple_of(i * ROWS, ROWS), ROWS)
        return pltpu.make_async_remote_copy(
            src_ref=back_sends.at[ex, rows, :],
            dst_ref=back_recvs.at[ex, rows, :],
            send_sem=bsend_sems.at[ex, i],
            recv_sem=brecv_sems.at[ex, i],
            device_id=at(xd, zd),
            device_id_type=MESH,
        )

    def each(copy_of, ex, action):
        def body(i, carry):
            copy = copy_of(ex, i)
            if action == "start":
                copy.start()
            elif action == "recv":
                copy.wait_recv()
            else:
                copy.wait_send()
            return carry

        lax.fori_loop(1, NB, body, 0)

    def weight_copy(n):
        src, dst = (
            (wgu, wgu_other),
            (wdn.at[0:128, :], wd_pair.at[128:256, :]),
            (wdn.at[128:192, :], wd_pair.at[320:384, :]),
        )[n]
        return pltpu.make_async_remote_copy(
            src_ref=src, dst_ref=dst, send_sem=w_send.at[n], recv_sem=w_recv.at[n],
            device_id=partner, device_id_type=MESH,
        )

    def hop_copy(n):
        return pltpu.make_async_remote_copy(
            src_ref=hop_out.at[n], dst_ref=hop_in.at[n], send_sem=hop_send.at[n], recv_sem=hop_recv.at[n],
            device_id=after if n == 0 else before, device_id_type=MESH,
        )

    sub = lax.broadcasted_iota(jnp.int32, (toks, toks), 0)
    lane = lax.broadcasted_iota(jnp.int32, (toks, toks), 1)

    def column(row):
        return jnp.sum(jnp.where(sub == lane, jnp.broadcast_to(row, (toks, toks)), 0), axis=1, keepdims=True)

    def place(ids):
        dx = (ids // 2 - x + XS) % XS
        other = (ids % 2 + own_half) % 2
        return dx, other

    def plan(step):
        row_ids = routes[step : step + 1, :]
        col_ids = column(row_ids)
        same = (col_ids == row_ids).astype(jnp.int32)
        rank_col = jnp.sum(jnp.where(lane < sub, same, 0), axis=1, keepdims=True)
        rank_row = jnp.sum(jnp.where(sub < lane, same, 0), axis=0, keepdims=True)
        dx_row, other_row = place(row_ids)
        block_row = dx_row * 2 + other_row
        slot_row = jnp.where(rank_row < ROWS, block_row * ROWS + rank_row, -1)
        pick = jnp.where(sub == slot_row, 1.0, 0.0).astype(BF16)
        spill_row = jnp.where(rank_row == ROWS, block_row, -1)
        spill_sub = lax.broadcasted_iota(jnp.int32, (16, toks), 0)
        pick_spill = jnp.where(spill_sub == spill_row, 1.0, 0.0).astype(BF16)
        dx_col, other_col = place(col_ids)
        first = dx_col * 4 + other_col * (3 - 2 * twist)
        second = dx_col * 4 + jnp.where(other_col == 1, 2, 1 + 2 * twist)
        wide = lax.broadcasted_iota(jnp.int32, (toks, NB * ROWS), 1)
        plain = rank_col < ROWS
        at_first = jnp.where(plain, first * ROWS + rank_col, -1)
        at_second = jnp.where(plain, second * ROWS + rank_col, -1)
        put = jnp.where(wide == at_first, 1.0, 0.0) + jnp.where(wide == at_second, 1.0, 0.0)
        narrow = lax.broadcasted_iota(jnp.int32, (toks, NB), 1)
        spill_first = jnp.where(plain, -1, first)
        spill_second = jnp.where(plain, -1, second)
        put_spill = jnp.where(narrow == spill_first, 1.0, 0.0) + jnp.where(narrow == spill_second, 1.0, 0.0)
        weight = column(mix[step : step + 1, :])
        return pick, pick_spill, put.astype(BF16), put_spill.astype(BF16), weight

    def dot(a, b):
        return jnp.dot(a, b, preferred_element_type=F32)

    def dot_t(a, b):
        return lax.dot_general(a, b, (((1,), (1,)), ((), ())), preferred_element_type=F32)

    def fold_rows(value, count):
        for c in range(chunks):
            fold[c // 8, pl.ds(c % 8, count, stride=8), :] = value[:count, c * LANES : (c + 1) * LANES]
        for c in range(chunks, folds * 8):
            fold[c // 8, pl.ds(c % 8, count, stride=8), :] = jnp.zeros((count, LANES), F32)

    def unfold_rows(buffer):
        for b in range(folds):
            fold[b] = buffer[:, width + b * LANES : width + (b + 1) * LANES].astype(F32)
        return jnp.concatenate([fold[c // 8, pl.ds(c % 8, NB, stride=8), :] for c in range(chunks)], axis=1)

    def dispatch(ex, step_plan, values):
        pick, pick_spill, _, _, _ = step_plan
        buffer = sends.at[ex]
        buffer[:, :width] = dot(pick, values).astype(BF16)
        fold_rows(dot(pick_spill, values), 8)
        for b in range(folds):
            buffer[:, width + b * LANES : width + (b + 1) * LANES] = fold[b, 0 : 8 * ROWS, :].astype(BF16)
        each(dispatch_copy, ex, "start")
        recvs[ex, 0:ROWS, :] = sends[ex, 0:ROWS, :]

    def arrived(ex):
        each(dispatch_copy, ex, "recv")
        buffer = recvs.at[ex]
        x_all[0 : NB * ROWS, :] = buffer[:, :width]
        x_all[NB * ROWS :, :] = unfold_rows(buffer).astype(BF16)

    def send_back(ex, value_of):
        buffer = back_sends.at[ex]
        value = value_of()
        buffer[:, :width] = value[: NB * ROWS].astype(BF16)
        fold_rows(value[NB * ROWS :], NB)
        for b in range(folds):
            buffer[:, width + b * LANES : width + (b + 1) * LANES] = fold[b].astype(BF16)
        each(back_copy, ex, "start")
        back_recvs[ex, 0:ROWS, :] = back_sends[ex, 0:ROWS, :]

    def collected(ex, step_plan):
        each(back_copy, ex, "recv")
        _, _, put, put_spill, weight = step_plan
        buffer = back_recvs.at[ex]
        spill = unfold_rows(buffer).astype(BF16)
        return weight * (dot(put, buffer[:, :width]) + dot(put_spill, spill))

    low = lax.broadcasted_iota(jnp.int32, (NB * (ROWS + 1), LANES), 1) < half

    def turn(value):
        return pltpu.roll(value, half, 1)

    def project(step, wait):
        own = dot(x_all[...], wgu[...])
        if wait:
            weight_copy(0).wait_recv()
        other = dot(x_all[...], wgu_other[...])
        gates[step, :, 0:128] = own[:, 0:128]
        gates[step, :, 128:256] = other[:, 0:128]
        gates[step, :, 256:384] = jnp.where(low, own[:, 256:384], turn(other[:, 256:384]))
        uppers[step, :, 0:128] = own[:, 128:256]
        uppers[step, :, 128:256] = other[:, 128:256]
        uppers[step, :, 256:384] = jnp.where(low, turn(own[:, 256:384]), other[:, 256:384])
        gate = gates[step]
        inner[...] = (gate * jax.nn.sigmoid(gate) * uppers[step]).astype(BF16)

    def expand():
        return dot(inner[...], wd_pair[...])

    def derive(step):
        d_inner = dot_t(x_all[...], wd_pair[...])
        gate = gates[step]
        r = jax.nn.sigmoid(gate)
        d_gate = d_inner * uppers[step] * r * (1.0 + gate * (1.0 - r))
        d_upper = d_inner * gate * r
        d_own[:, 0:128] = d_gate[:, 0:128].astype(BF16)
        d_own[:, 128:256] = d_upper[:, 0:128].astype(BF16)
        d_own[:, 256:384] = jnp.where(low, d_gate[:, 256:384], turn(d_upper[:, 256:384])).astype(BF16)
        d_other[:, 0:128] = d_gate[:, 128:256].astype(BF16)
        d_other[:, 128:256] = d_upper[:, 128:256].astype(BF16)
        d_other[:, 256:384] = jnp.where(low, turn(d_gate[:, 256:384]), d_upper[:, 256:384]).astype(BF16)

    def contract():
        return dot_t(d_own[...], wgu[...]) + dot_t(d_other[...], wgu_other[...])

    def inv_scale(values):
        return lax.rsqrt(jnp.mean(values * values, axis=-1, keepdims=True) + EPSILON)

    def normed(hidden):
        values = hidden.astype(F32)
        return (values * inv_scale(values) * gain[...]).astype(BF16)

    def pulled(hidden, grad, d_normed):
        values = hidden.astype(F32)
        r = inv_scale(values)
        scaled = d_normed * gain[...]
        mean = jnp.mean(scaled * values, axis=-1, keepdims=True)
        return grad.astype(F32) + r * scaled - values * (r * r * r * mean)

    plan0 = plan(0)
    plan1 = plan(1)
    first_rows = normed(tokens[...])
    pl.semaphore_wait(barrier, 2 * (NB - 1) + 3)

    dispatch(0, plan0, first_rows)
    for n in range(3):
        weight_copy(n).start()
    wd_pair[0:128, :] = wdn[0:128, :]
    wd_pair[256:320, :] = wdn[128:192, :]
    arrived(0)
    project(0, True)
    weight_copy(1).wait_recv()
    weight_copy(2).wait_recv()
    send_back(0, expand)
    dispatch(1, plan1, cotangent[...])
    hop_out[0] = (tokens[...].astype(F32) + collected(0, plan0)).astype(BF16)
    hop_copy(0).start()
    hop_copy(0).wait_recv()
    hidden1[...] = hop_in[0]
    dispatch(2, plan1, normed(hidden1[...]))
    arrived(2)
    project(1, False)
    arrived(1)
    derive(1)
    send_back(1, contract)
    send_back(2, expand)
    grad1 = pulled(hidden1[...], cotangent[...], collected(1, plan1))
    hop_out[1] = grad1.astype(BF16)
    hop_copy(1).start()
    final[...] = (hidden1[...].astype(F32) + collected(2, plan1)).astype(BF16)
    hop_copy(1).wait_recv()
    dispatch(3, plan0, hop_in[1])
    arrived(3)
    derive(0)
    send_back(3, contract)
    grads[...] = pulled(tokens[...], hop_in[1], collected(3, plan0)).astype(BF16)

    for ex in range(4):
        each(dispatch_copy, ex, "sent")
        each(back_copy, ex, "sent")
    for n in range(3):
        weight_copy(n).wait_send()
    for n in range(2):
        hop_copy(n).wait_send()


def local(tokens, norm_gain, w_gate, w_up, w_down, routes, mix_weights, cotangent):
    toks, width = tokens.shape[1:]
    hid = w_gate.shape[3]
    gate_w, up_w = w_gate[0, 0], w_up[0, 0]
    packed = jnp.concatenate([gate_w[:, :128], up_w[:, :128], gate_w[:, 128:], up_w[:, 128:]], axis=1)
    lanes = width + 3 * LANES
    rows = NB * (ROWS + 1)
    dma = pltpu.SemaphoreType.DMA
    vmem = pl.BlockSpec(memory_space=pltpu.VMEM)
    out = jax.ShapeDtypeStruct((toks, width), BF16)
    final, grads = pl.pallas_call(
        kernel,
        out_shape=(out, out),
        in_specs=[vmem] * 7,
        out_specs=(vmem, vmem),
        scratch_shapes=[
            pltpu.VMEM((width, 2 * hid), BF16),
            pltpu.VMEM((2 * hid, width), BF16),
            pltpu.VMEM((4, 8 * ROWS, lanes), BF16),
            pltpu.VMEM((4, NB * ROWS, lanes), BF16),
            pltpu.VMEM((4, NB * ROWS, lanes), BF16),
            pltpu.VMEM((4, NB * ROWS, lanes), BF16),
            pltpu.VMEM((3, NB * ROWS, LANES), F32),
            pltpu.VMEM((rows, width), BF16),
            pltpu.VMEM((2, rows, 2 * hid), F32),
            pltpu.VMEM((2, rows, 2 * hid), F32),
            pltpu.VMEM((toks, width), BF16),
            pltpu.VMEM((2, toks, width), BF16),
            pltpu.VMEM((2, toks, width), BF16),
            pltpu.VMEM((rows, 2 * hid), BF16),
            pltpu.VMEM((rows, 2 * hid), BF16),
            pltpu.VMEM((rows, 2 * hid), BF16),
            dma((4, NB)),
            dma((4, NB)),
            dma((4, NB)),
            dma((4, NB)),
            dma((3,)),
            dma((3,)),
            dma((2,)),
            dma((2,)),
        ],
        compiler_params=pltpu.CompilerParams(
            collective_id=0, has_side_effects=True, vmem_limit_bytes=56 * 1024 * 1024
        ),
    )(
        tokens[0], norm_gain, packed, w_down[0, 0],
        routes[0, :, :, 0], mix_weights[0, :, :, 0], cotangent[0],
    )
    return final[None], grads[None]


def solution(mesh):
    in_specs = (
        P("section", "expert", None),
        P("section", None),
        P("section", "expert", None, None),
        P("section", "expert", None, None),
        P("section", "expert", None, None),
        P("section", None, "expert", None),
        P("section", None, "expert", None),
        P("section", "expert", None),
    )
    out_specs = (P("section", "expert", None), P("section", "expert", None))
    return jax.shard_map(local, mesh=mesh, in_specs=in_specs, out_specs=out_specs, check_vma=False)
```

time: 609 us -> 230 us (0.38)
  the two profiles are of different devices: /device:TPU:88 before, /device:TPU:24 now
where the time goes in v1:
time: 230 us
  Pallas kernels  221 us (96%)
  local copies, waits for them, and re-layouts  6.69 us (3%)
    pallas_call x1, Pallas kernels, local(): pl.pallas_call(kernel, out_shape=(out, out), in_specs=[vmem] * 7, out_spe...  221 us
    unnamed x4, local copies, waits for them, and re-layouts  6.51 us

profile of v1, /device:TPU:24, one launch (start us, length us, event | category | flops | bytes accessed | tf_op | source)
XLA Modules:
  0.0 230.0 jit_solution(15654909995252815137)
XLA Ops:
  0.6 1.5 copy.10
  2.3 1.5 copy.11
  3.9 1.8 pad_maximum_fusion.wgu
  5.7 220.9 %shard_map.95 = (bf16[64,2560]{1,0:T(8,128)(2,1)}, bf16[64,2560]{1,0:T(8,128)(2,1)}) custom-call(bf16[64,2560]{1,0:T(8,128)(2,1)} %bitcast.16, f32[1,2560]{1,0:T(1,128)} %gain.1, bf16[2560,384]{1,0:T(8,128)(2,1)} %pad_maximum_fusion.wgu, bf16[192,2560]{1,0:T(8,128)(2,1)} %bitcast.13, s32[2,64]{1,0:T(2,128)} %bitcast.18, f32[2,64]{1,0:T(2,128)} %bitcast.19, ...), custom_call_target="tpu_custom_call" | custom-call | tf_op jit(solution)/shard_map/pallas_call | solution.py:325
  226.6 1.7 copy.14
  228.3 1.7 copy.15
  (4 shorter events, 0.2 us)

commit v2 on v1

v2 whole, which is shorter than its diff:
```python
import jax
import jax.numpy as jnp
from jax import lax
from jax.experimental import pallas as pl
from jax.experimental.pallas import tpu as pltpu
from jax.sharding import PartitionSpec as P

MESH = pl.DeviceIdType.MESH
EPSILON = 1e-06
F32 = jnp.float32
BF16 = jnp.bfloat16
XS = 4
ZS = 8
NB = 16
ROWS = 8
LANES = 128
SELF = 12
FAR, NEAR = ((0, 8),), ((8, SELF), (SELF + 1, NB))
ALL = ((0, SELF), (SELF + 1, NB))
CUT = 64


def kernel(
    tokens, gain, w_gate, w_up, w_down, routes, mix, cotangent, final, grads,
    wg, wu, wd, sends, recvs, back_sends, back_recvs, fold, x_all, gates, uppers, hidden1,
    hop_out, hop_in, d_gates, d_uppers,
    send_sems, recv_sems, bsend_sems, brecv_sems, w_local, w_send, w_recv, hop_send, hop_recv,
):
    width = tokens.shape[1]
    toks = tokens.shape[0]
    hid = w_gate.shape[0]
    chunks = width // LANES
    folds = -(-chunks // 8)
    section = lax.axis_index("section")
    sections = lax.axis_size("section")
    me = lax.axis_index("expert")
    x = me // ZS
    z = me % ZS
    sign = 1 - 2 * (z % 2)
    own_half = z // 4
    twist = ((z + 1) // 2) % 2

    def at(xd, zd):
        return {"expert": ((xd + XS) % XS) * ZS + (zd + 2 * ZS) % ZS}

    def target(i):
        j = i // 4
        off = (j - 3) * (1 - 2 * (j % 2))
        return x + i % 4, (z + off * sign + ZS) % ZS

    def origin(i):
        return x - i % 4, (z + (i // 4 - 3) * sign + ZS) % ZS

    partner = at(x, z + sign)
    after = {"section": (section + 1) % sections}
    before = {"section": (section + sections - 1) % sections}

    def weight_local(n):
        src, dst = ((w_gate, wg), (w_up, wu), (w_down, wd))[n]
        return pltpu.make_async_copy(src, dst.at[0:hid, :], w_local.at[n])

    def weight_copy(n):
        src, dst = ((w_gate, wg), (w_up, wu), (w_down, wd))[n]
        return pltpu.make_async_remote_copy(
            src_ref=src, dst_ref=dst.at[hid : 2 * hid, :], send_sem=w_send.at[n], recv_sem=w_recv.at[n],
            device_id=partner, device_id_type=MESH,
        )

    def hop_copy(n):
        return pltpu.make_async_remote_copy(
            src_ref=hop_out.at[n], dst_ref=hop_in.at[n], send_sem=hop_send.at[n], recv_sem=hop_recv.at[n],
            device_id=after if n == 0 else before, device_id_type=MESH,
        )

    def over(ranges, action):
        def body(i, carry):
            action(i)
            return carry

        for low, high in ranges:
            lax.fori_loop(low, high, body, 0)

    barrier = pltpu.get_barrier_semaphore()

    def greet(place_of):
        def action(i):
            xd, zd = place_of(i)
            pl.semaphore_signal(barrier, inc=1, device_id=at(xd, zd), device_id_type=MESH)

        over(ALL, action)

    greet(target)
    greet(origin)
    for neighbour in (partner, after, before):
        pl.semaphore_signal(barrier, inc=1, device_id=neighbour, device_id_type=MESH)
    for n in range(3):
        weight_local(n).start()

    def dispatch_copy(ex, i):
        xd, zd = target(i)
        block = (i % 4) * 2 + (zd // 4 + own_half) % 2
        return pltpu.make_async_remote_copy(
            src_ref=sends.at[ex, pl.ds(pl.multiple_of(block * ROWS, ROWS), ROWS), :],
            dst_ref=recvs.at[ex, pl.ds(pl.multiple_of(i * ROWS, ROWS), ROWS), :],
            send_sem=send_sems.at[ex, i],
            recv_sem=recv_sems.at[ex, i],
            device_id=at(xd, zd),
            device_id_type=MESH,
        )

    def back_copy(ex, i):
        xd, zd = origin(i)
        rows = pl.ds(pl.multiple_of(i * ROWS, ROWS), ROWS)
        return pltpu.make_async_remote_copy(
            src_ref=back_sends.at[ex, rows, :],
            dst_ref=back_recvs.at[ex, rows, :],
            send_sem=bsend_sems.at[ex, i],
            recv_sem=brecv_sems.at[ex, i],
            device_id=at(xd, zd),
            device_id_type=MESH,
        )

    def each(copy_of, ex, action, ranges):
        def one(i):
            copy = copy_of(ex, i)
            if action == "start":
                copy.start()
            elif action == "recv":
                copy.wait_recv()
            else:
                copy.wait_send()

        over(ranges, one)

    sub = lax.broadcasted_iota(jnp.int32, (toks, toks), 0)
    lane = lax.broadcasted_iota(jnp.int32, (toks, toks), 1)

    def column(row):
        return jnp.sum(jnp.where(sub == lane, jnp.broadcast_to(row, (toks, toks)), 0), axis=1, keepdims=True)

    def place(ids):
        dx = (ids // 2 - x + XS) % XS
        other = (ids % 2 + own_half) % 2
        return dx, other

    def plan(step):
        row_ids = routes[step : step + 1, :]
        col_ids = column(row_ids)
        same = (col_ids == row_ids).astype(jnp.int32)
        rank_col = jnp.sum(jnp.where(lane < sub, same, 0), axis=1, keepdims=True)
        rank_row = jnp.sum(jnp.where(sub < lane, same, 0), axis=0, keepdims=True)
        dx_row, other_row = place(row_ids)
        block_row = dx_row * 2 + other_row
        slot_row = jnp.where(rank_row < ROWS, block_row * ROWS + rank_row, -1)
        pick = jnp.where(sub == slot_row, 1.0, 0.0).astype(BF16)
        spill_row = jnp.where(rank_row == ROWS, block_row, -1)
        spill_sub = lax.broadcasted_iota(jnp.int32, (16, toks), 0)
        pick_spill = jnp.where(spill_sub == spill_row, 1.0, 0.0).astype(BF16)
        dx_col, other_col = place(col_ids)
        first = jnp.where(other_col == 1, 0, 12) + dx_col
        second = jnp.where(other_col == 1, 2 - twist, 1 + twist) * 4 + dx_col
        wide = lax.broadcasted_iota(jnp.int32, (toks, NB * ROWS), 1)
        plain = rank_col < ROWS
        at_first = jnp.where(plain, first * ROWS + rank_col, -1)
        at_second = jnp.where(plain, second * ROWS + rank_col, -1)
        put = jnp.where(wide == at_first, 1.0, 0.0) + jnp.where(wide == at_second, 1.0, 0.0)
        narrow = lax.broadcasted_iota(jnp.int32, (toks, NB), 1)
        spill_first = jnp.where(plain, -1, first)
        spill_second = jnp.where(plain, -1, second)
        put_spill = jnp.where(narrow == spill_first, 1.0, 0.0) + jnp.where(narrow == spill_second, 1.0, 0.0)
        weight = column(mix[step : step + 1, :])
        return pick, pick_spill, put.astype(BF16), put_spill.astype(BF16), weight

    def dot(a, b):
        return jnp.dot(a, b, preferred_element_type=F32)

    def dot_t(a, b):
        return lax.dot_general(a, b, (((1,), (1,)), ((), ())), preferred_element_type=F32)

    def fold_rows(value, count, buffer, rows):
        for c in range(chunks):
            fold[c // 8, pl.ds(c % 8, count, stride=8), :] = value[:count, c * LANES : (c + 1) * LANES]
        for c in range(chunks, folds * 8):
            fold[c // 8, pl.ds(c % 8, count, stride=8), :] = jnp.zeros((count, LANES), F32)
        for b in range(folds):
            buffer[0:rows, width + b * LANES : width + (b + 1) * LANES] = fold[b, 0:rows, :].astype(BF16)

    def unfold_rows(buffer):
        for b in range(folds):
            fold[b] = buffer[:, width + b * LANES : width + (b + 1) * LANES].astype(F32)
        return jnp.concatenate([fold[c // 8, pl.ds(c % 8, NB, stride=8), :] for c in range(chunks)], axis=1)

    def pack(ex, step_plan, values):
        pick, pick_spill, _, _, _ = step_plan
        buffer = sends.at[ex]
        buffer[:, :width] = dot(pick, values).astype(BF16)
        fold_rows(dot(pick_spill, values), 8, buffer, 8 * ROWS)
        recvs[ex, SELF * ROWS : (SELF + 1) * ROWS, :] = sends[ex, 0:ROWS, :]

    def arrived(ex):
        each(dispatch_copy, ex, "recv", ALL)
        buffer = recvs.at[ex]
        x_all[0:CUT, :] = buffer[0:CUT, :width]
        x_all[CUT : CUT + NB, :] = unfold_rows(buffer).astype(BF16)
        x_all[CUT + NB :, :] = buffer[CUT:, :width]

    def send_back(ex, value_of, start):
        buffer = back_sends.at[ex]
        value = value_of(slice(0, CUT + NB))
        buffer[0:CUT, :width] = value[:CUT].astype(BF16)
        fold_rows(value[CUT:], NB, buffer, NB * ROWS)
        if start:
            each(back_copy, ex, "start", FAR)
        buffer[CUT:, :width] = value_of(slice(CUT + NB, NB * (ROWS + 1))).astype(BF16)
        if start:
            each(back_copy, ex, "start", NEAR)
        back_recvs[ex, SELF * ROWS : (SELF + 1) * ROWS, :] = back_sends[ex, SELF * ROWS : (SELF + 1) * ROWS, :]

    def collected(ex, step_plan):
        each(back_copy, ex, "recv", ALL)
        _, _, put, put_spill, weight = step_plan
        buffer = back_recvs.at[ex]
        spill = unfold_rows(buffer).astype(BF16)
        return weight * (dot(put, buffer[:, :width]) + dot(put_spill, spill))

    def activate(step):
        gate = gates[step]
        d_gates[...] = (gate * jax.nn.sigmoid(gate) * uppers[step]).astype(BF16)

    def expand(rows):
        return dot(d_gates[rows, :], wd[...])

    def derive(step):
        d_inner = dot_t(x_all[...], wd[...])
        gate = gates[step]
        r = jax.nn.sigmoid(gate)
        d_gates[...] = (d_inner * uppers[step] * r * (1.0 + gate * (1.0 - r))).astype(BF16)
        d_uppers[...] = (d_inner * gate * r).astype(BF16)

    def contract(rows):
        return dot(d_gates[rows, :], wg[...]) + dot(d_uppers[rows, :], wu[...])

    def inv_scale(values):
        return lax.rsqrt(jnp.mean(values * values, axis=-1, keepdims=True) + EPSILON)

    def normed(hidden):
        values = hidden.astype(F32)
        return (values * inv_scale(values) * gain[...]).astype(BF16)

    def pulled(hidden, grad, d_normed):
        values = hidden.astype(F32)
        r = inv_scale(values)
        scaled = d_normed * gain[...]
        mean = jnp.mean(scaled * values, axis=-1, keepdims=True)
        return grad.astype(F32) + r * scaled - values * (r * r * r * mean)

    plan0 = plan(0)
    pack(0, plan0, normed(tokens[...]))
    pl.semaphore_wait(barrier, 2 * (NB - 1) + 3)
    weight_copy(0).start()
    weight_copy(1).start()
    each(dispatch_copy, 0, "start", ALL)
    plan1 = plan(1)
    pack(1, plan1, cotangent[...])
    each(dispatch_copy, 1, "start", NEAR)
    for n in range(3):
        weight_local(n).wait()
    arrived(0)
    weight_copy(2).start()
    weight_copy(0).wait_recv()
    gates[0] = dot_t(x_all[...], wg[...])
    weight_copy(1).wait_recv()
    uppers[0] = dot_t(x_all[...], wu[...])
    activate(0)
    weight_copy(2).wait_recv()
    send_back(0, expand, True)
    hop_out[0] = (tokens[...].astype(F32) + collected(0, plan0)).astype(BF16)
    hop_copy(0).start()
    each(dispatch_copy, 1, "start", FAR)
    hop_copy(0).wait_recv()
    hidden1[...] = hop_in[0]
    pack(2, plan1, normed(hidden1[...]))
    each(dispatch_copy, 2, "start", ALL)
    arrived(2)
    gates[1] = dot_t(x_all[...], wg[...])
    uppers[1] = dot_t(x_all[...], wu[...])
    arrived(1)
    derive(1)
    send_back(1, contract, True)
    activate(1)
    send_back(2, expand, False)
    grad1 = pulled(hidden1[...], cotangent[...], collected(1, plan1))
    hop_out[1] = grad1.astype(BF16)
    hop_copy(1).start()
    each(back_copy, 2, "start", ALL)
    hop_copy(1).wait_recv()
    pack(3, plan0, hop_in[1])
    each(dispatch_copy, 3, "start", ALL)
    final[...] = (hidden1[...].astype(F32) + collected(2, plan1)).astype(BF16)
    arrived(3)
    derive(0)
    send_back(3, contract, True)
    grads[...] = pulled(tokens[...], hop_in[1], collected(3, plan0)).astype(BF16)

    for ex in range(4):
        each(dispatch_copy, ex, "sent", ALL)
        each(back_copy, ex, "sent", ALL)
    for n in range(3):
        weight_copy(n).wait_send()
    for n in range(2):
        hop_copy(n).wait_send()


def local(tokens, norm_gain, w_gate, w_up, w_down, routes, mix_weights, cotangent):
    toks, width = tokens.shape[1:]
    hid = w_gate.shape[3]
    lanes = width + 3 * LANES
    rows = NB * (ROWS + 1)
    dma = pltpu.SemaphoreType.DMA
    vmem = pl.BlockSpec(memory_space=pltpu.VMEM)
    anywhere = pl.BlockSpec(memory_space=pl.ANY)
    out = jax.ShapeDtypeStruct((toks, width), BF16)
    final, grads = pl.pallas_call(
        kernel,
        out_shape=(out, out),
        in_specs=[vmem] * 2 + [anywhere] * 3 + [vmem] * 3,
        out_specs=(vmem, vmem),
        scratch_shapes=[
            pltpu.VMEM((2 * hid, width), BF16),
            pltpu.VMEM((2 * hid, width), BF16),
            pltpu.VMEM((2 * hid, width), BF16),
            pltpu.VMEM((4, 8 * ROWS, lanes), BF16),
            pltpu.VMEM((4, NB * ROWS, lanes), BF16),
            pltpu.VMEM((4, NB * ROWS, lanes), BF16),
            pltpu.VMEM((4, NB * ROWS, lanes), BF16),
            pltpu.VMEM((3, NB * ROWS, LANES), F32),
            pltpu.VMEM((rows, width), BF16),
            pltpu.VMEM((2, rows, 2 * hid), F32),
            pltpu.VMEM((2, rows, 2 * hid), F32),
            pltpu.VMEM((toks, width), BF16),
            pltpu.VMEM((2, toks, width), BF16),
            pltpu.VMEM((2, toks, width), BF16),
            pltpu.VMEM((rows, 2 * hid), BF16),
            pltpu.VMEM((rows, 2 * hid), BF16),
            dma((4, NB)),
            dma((4, NB)),
            dma((4, NB)),
            dma((4, NB)),
            dma((3,)),
            dma((3,)),
            dma((3,)),
            dma((2,)),
            dma((2,)),
        ],
        compiler_params=pltpu.CompilerParams(
            collective_id=0, has_side_effects=True, vmem_limit_bytes=56 * 1024 * 1024
        ),
    )(
        tokens[0], norm_gain, w_gate[0, 0].T, w_up[0, 0].T, w_down[0, 0],
        routes[0, :, :, 0], mix_weights[0, :, :, 0], cotangent[0],
    )
    return final[None], grads[None]


def solution(mesh):
    in_specs = (
        P("section", "expert", None),
        P("section", None),
        P("section", "expert", None, None),
        P("section", "expert", None, None),
        P("section", "expert", None, None),
        P("section", None, "expert", None),
        P("section", None, "expert", None),
        P("section", "expert", None),
    )
    out_specs = (P("section", "expert", None), P("section", "expert", None))
    return jax.shard_map(local, mesh=mesh, in_specs=in_specs, out_specs=out_specs, check_vma=False)
```

time: 230 us -> 228 us (level)
  the two profiles are of different devices: /device:TPU:24 before, /device:TPU:312 now
where the time goes in v2:
time: 228 us
  Pallas kernels  225 us (99%)
  local copies, waits for them, and re-layouts  2.49 us (1%)
    pallas_call x1, Pallas kernels, local(): pl.pallas_call(kernel, out_shape=(out, out), in_specs=[vmem] * 2 + [anywh...  225 us

profile of v2, /device:TPU:312, one launch (start us, length us, event | category | flops | bytes accessed | tf_op | source)
XLA Modules:
  0.0 228.1 jit_solution(13986739281852198391)
XLA Ops:
  0.6 224.9 %shard_map.95 = (bf16[64,2560]{1,0:T(8,128)(2,1)}, bf16[64,2560]{1,0:T(8,128)(2,1)}) custom-call(bf16[64,2560]{1,0:T(8,128)(2,1)} %bitcast.18, f32[1,2560]{1,0:T(1,128)} %gain.1, bf16[192,2560]{1,0:T(8,128)(2,1)} %bitcast.13, bf16[192,2560]{1,0:T(8,128)(2,1)} %bitcast.14, bf16[192,2560]{1,0:T(8,128)(2,1)} %bitcast.15, s32[2,64]{1,0:T(2,128)} %bitcast.20, ...), custom_call_target="tpu_custom_call" | custom-call | tf_op jit(solution)/shard_map/pallas_call | solution.py:323
  225.6 0.0 copy-start
  225.6 1.8 copy.12
  227.4 0.0 copy-done
  227.4 0.7 copy.13
Async XLA Ops:
  225.6 1.8 copy-start

commit v3 on v2

--- a/solution.py
+++ b/solution.py
@@ -17,14 +17,15 @@
 SELF = 12
 FAR, NEAR = ((0, 8),), ((8, SELF), (SELF + 1, NB))
 ALL = ((0, SELF), (SELF + 1, NB))
-CUT = 64
+PARTS = (FAR, NEAR)
+HALF = 8
 
 
 def kernel(
     tokens, gain, w_gate, w_up, w_down, routes, mix, cotangent, final, grads,
     wg, wu, wd, sends, recvs, back_sends, back_recvs, fold, x_all, gates, uppers, hidden1,
-    hop_out, hop_in, d_gates, d_uppers,
-    send_sems, recv_sems, bsend_sems, brecv_sems, w_local, w_send, w_recv, hop_send, hop_recv,
+    hop_out, hop_in,
+    send_sems, recv_sems, bsend_sems, brecv_sems, w_send, w_recv, hop_send, hop_recv,
 ):
     width = tokens.shape[1]
     toks = tokens.shape[0]
@@ -55,10 +56,6 @@
     after = {"section": (section + 1) % sections}
     before = {"section": (section + sections - 1) % sections}
 
-    def weight_local(n):
-        src, dst = ((w_gate, wg), (w_up, wu), (w_down, wd))[n]
-        return pltpu.make_async_copy(src, dst.at[0:hid, :], w_local.at[n])
-
     def weight_copy(n):
         src, dst = ((w_gate, wg), (w_up, wu), (w_down, wd))[n]
         return pltpu.make_async_remote_copy(
@@ -93,8 +90,6 @@
     greet(origin)
     for neighbour in (partner, after, before):
         pl.semaphore_signal(barrier, inc=1, device_id=neighbour, device_id_type=MESH)
-    for n in range(3):
-        weight_local(n).start()
 
     def dispatch_copy(ex, i):
         xd, zd = target(i)
@@ -159,17 +154,23 @@
         dx_col, other_col = place(col_ids)
         first = jnp.where(other_col == 1, 0, 12) + dx_col
         second = jnp.where(other_col == 1, 2 - twist, 1 + twist) * 4 + dx_col
-        wide = lax.broadcasted_iota(jnp.int32, (toks, NB * ROWS), 1)
         plain = rank_col < ROWS
-        at_first = jnp.where(plain, first * ROWS + rank_col, -1)
-        at_second = jnp.where(plain, second * ROWS + rank_col, -1)
-        put = jnp.where(wide == at_first, 1.0, 0.0) + jnp.where(wide == at_second, 1.0, 0.0)
-        narrow = lax.broadcasted_iota(jnp.int32, (toks, NB), 1)
-        spill_first = jnp.where(plain, -1, first)
-        spill_second = jnp.where(plain, -1, second)
-        put_spill = jnp.where(narrow == spill_first, 1.0, 0.0) + jnp.where(narrow == spill_second, 1.0, 0.0)
+        wide = lax.broadcasted_iota(jnp.int32, (toks, HALF * ROWS), 1)
+        narrow = lax.broadcasted_iota(jnp.int32, (toks, HALF), 1)
+        puts, put_spills = [], []
+        for part in range(2):
+            begin = part * HALF
+            put, put_spill = 0.0, 0.0
+            for block in (first, second):
+                inside = (block >= begin) & (block < begin + HALF)
+                slot = jnp.where(plain & inside, (block - begin) * ROWS + rank_col, -1)
+                put = put + jnp.where(wide == slot, 1.0, 0.0)
+                slot = jnp.where(plain, -1, block - begin)
+                put_spill = put_spill + jnp.where(narrow == slot, 1.0, 0.0)
+            puts.append(put.astype(BF16))
+            put_spills.append(put_spill.astype(BF16))
         weight = column(mix[step : step + 1, :])
-        return pick, pick_spill, put.astype(BF16), put_spill.astype(BF16), weight
+        return pick, pick_spill, puts, put_spills, weight
 
     def dot(a, b):
         return jnp.dot(a, b, preferred_element_type=F32)
@@ -177,68 +178,70 @@
     def dot_t(a, b):
         return lax.dot_general(a, b, (((1,), (1,)), ((), ())), preferred_element_type=F32)
 
-    def fold_rows(value, count, buffer, rows):
+    def fold_rows(value, buffer):
         for c in range(chunks):
-            fold[c // 8, pl.ds(c % 8, count, stride=8), :] = value[:count, c * LANES : (c + 1) * LANES]
+            fold[c // 8, pl.ds(c % 8, 8, stride=8), :] = value[:8, c * LANES : (c + 1) * LANES]
         for c in range(chunks, folds * 8):
-            fold[c // 8, pl.ds(c % 8, count, stride=8), :] = jnp.zeros((count, LANES), F32)
+            fold[c // 8, pl.ds(c % 8, 8, stride=8), :] = jnp.zeros((8, LANES), F32)
         for b in range(folds):
-            buffer[0:rows, width + b * LANES : width + (b + 1) * LANES] = fold[b, 0:rows, :].astype(BF16)
+            buffer[:, width + b * LANES : width + (b + 1) * LANES] = fold[b].astype(BF16)
 
     def unfold_rows(buffer):
         for b in range(folds):
             fold[b] = buffer[:, width + b * LANES : width + (b + 1) * LANES].astype(F32)
-        return jnp.concatenate([fold[c // 8, pl.ds(c % 8, NB, stride=8), :] for c in range(chunks)], axis=1)
+        return jnp.concatenate([fold[c // 8, pl.ds(c % 8, 8, stride=8), :] for c in range(chunks)], axis=1)
 
     def pack(ex, step_plan, values):
         pick, pick_spill, _, _, _ = step_plan
         buffer = sends.at[ex]
         buffer[:, :width] = dot(pick, values).astype(BF16)
-        fold_rows(dot(pick_spill, values), 8, buffer, 8 * ROWS)
+        fold_rows(dot(pick_spill, values), buffer)
         recvs[ex, SELF * ROWS : (SELF + 1) * ROWS, :] = sends[ex, 0:ROWS, :]
 
-    def arrived(ex):
-        each(dispatch_copy, ex, "recv", ALL)
-        buffer = recvs.at[ex]
-        x_all[0:CUT, :] = buffer[0:CUT, :width]
-        x_all[CUT : CUT + NB, :] = unfold_rows(buffer).astype(BF16)
-        x_all[CUT + NB :, :] = buffer[CUT:, :width]
-
-    def send_back(ex, value_of, start):
-        buffer = back_sends.at[ex]
-        value = value_of(slice(0, CUT + NB))
-        buffer[0:CUT, :width] = value[:CUT].astype(BF16)
-        fold_rows(value[CUT:], NB, buffer, NB * ROWS)
+    def part_rows(part):
+        return slice(part * HALF * ROWS, (part + 1) * HALF * ROWS)
+
+    def arrived(ex, part):
+        each(dispatch_copy, ex, "recv", PARTS[part])
+        buffer = recvs.at[ex, part_rows(part), :]
+        x_all[part, 0 : HALF * ROWS, :] = buffer[:, :width]
+        x_all[part, HALF * ROWS : HALF * ROWS + 8, :] = unfold_rows(buffer).astype(BF16)
+
+    def send_back(ex, part, value, start):
+        buffer = back_sends.at[ex, part_rows(part), :]
+        buffer[:, :width] = value[: HALF * ROWS].astype(BF16)
+        fold_rows(value[HALF * ROWS :], buffer)
         if start:
-            each(back_copy, ex, "start", FAR)
-        buffer[CUT:, :width] = value_of(slice(CUT + NB, NB * (ROWS + 1))).astype(BF16)
-        if start:
-            each(back_copy, ex, "start", NEAR)
-        back_recvs[ex, SELF * ROWS : (SELF + 1) * ROWS, :] = back_sends[ex, SELF * ROWS : (SELF + 1) * ROWS, :]
+            each(back_copy, ex, "start", PARTS[part])
+        if part == 1:
+            back_recvs[ex, SELF * ROWS : (SELF + 1) * ROWS, :] = back_sends[ex, SELF * ROWS : (SELF + 1) * ROWS, :]
 
     def collected(ex, step_plan):
-        each(back_copy, ex, "recv", ALL)
-        _, _, put, put_spill, weight = step_plan
-        buffer = back_recvs.at[ex]
-        spill = unfold_rows(buffer).astype(BF16)
-        return weight * (dot(put, buffer[:, :width]) + dot(put_spill, spill))
-
-    def activate(step):
-        gate = gates[step]
-        d_gates[...] = (gate * jax.nn.sigmoid(gate) * uppers[step]).astype(BF16)
-
-    def expand(rows):
-        return dot(d_gates[rows, :], wd[...])
-
-    def derive(step):
-        d_inner = dot_t(x_all[...], wd[...])
-        gate = gates[step]
+        _, _, puts, put_spills, weight = step_plan
+        total = None
+        for part in (1, 0):
+            each(back_copy, ex, "recv", PARTS[part])
+            buffer = back_recvs.at[ex, part_rows(part), :]
+            spill = unfold_rows(buffer).astype(BF16)
+            term = dot(puts[part], buffer[:, :width]) + dot(put_spills[part], spill)
+            total = term if total is None else total + term
+        return weight * total
+
+    def project(step, part):
+        gates[step, part] = dot_t(x_all[part], wg[...])
+        uppers[step, part] = dot_t(x_all[part], wu[...])
+
+    def expand(step, part):
+        gate = gates[step, part]
+        return dot((gate * jax.nn.sigmoid(gate) * uppers[step, part]).astype(BF16), wd[...])
+
+    def derive(step, part):
+        d_inner = dot_t(x_all[part], wd[...])
+        gate = gates[step, part]
         r = jax.nn.sigmoid(gate)
-        d_gates[...] = (d_inner * uppers[step] * r * (1.0 + gate * (1.0 - r))).astype(BF16)
-        d_uppers[...] = (d_inner * gate * r).astype(BF16)
-
-    def contract(rows):
-        return dot(d_gates[rows, :], wg[...]) + dot(d_uppers[rows, :], wu[...])
+        d_gate = (d_inner * uppers[step, part] * r * (1.0 + gate * (1.0 - r))).astype(BF16)
+        d_upper = (d_inner * gate * r).astype(BF16)
+        return dot(d_gate, wg[...]) + dot(d_upper, wu[...])
 
     def inv_scale(values):
         return lax.rsqrt(jnp.mean(values * values, axis=-1, keepdims=True) + EPSILON)
@@ -263,17 +266,19 @@
     plan1 = plan(1)
     pack(1, plan1, cotangent[...])
     each(dispatch_copy, 1, "start", NEAR)
-    for n in range(3):
-        weight_local(n).wait()
-    arrived(0)
+    for own, pair in ((w_gate, wg), (w_up, wu), (w_down, wd)):
+        pair[0:hid, :] = own[...]
+    x_all[:, HALF * ROWS + 8 :, :] = jnp.zeros((2, 8, width), BF16)
+    arrived(0, 1)
+    arrived(0, 0)
     weight_copy(2).start()
     weight_copy(0).wait_recv()
-    gates[0] = dot_t(x_all[...], wg[...])
     weight_copy(1).wait_recv()
-    uppers[0] = dot_t(x_all[...], wu[...])
-    activate(0)
+    project(0, 0)
+    project(0, 1)
     weight_copy(2).wait_recv()
-    send_back(0, expand, True)
+    send_back(0, 0, expand(0, 0), True)
+    send_back(0, 1, expand(0, 1), True)
     hop_out[0] = (tokens[...].astype(F32) + collected(0, plan0)).astype(BF16)
     hop_copy(0).start()
     each(dispatch_copy, 1, "start", FAR)
@@ -281,25 +286,27 @@
     hidden1[...] = hop_in[0]
     pack(2, plan1, normed(hidden1[...]))
     each(dispatch_copy, 2, "start", ALL)
-    arrived(2)
-    gates[1] = dot_t(x_all[...], wg[...])
-    uppers[1] = dot_t(x_all[...], wu[...])
-    arrived(1)
-    derive(1)
-    send_back(1, contract, True)
-    activate(1)
-    send_back(2, expand, False)
+    for part in (1, 0):
+        arrived(2, part)
+        project(1, part)
+        arrived(1, part)
+        send_back(1, part, derive(1, part), True)
+    send_back(2, 1, expand(1, 1), False)
+    send_back(2, 0, expand(1, 0), False)
     grad1 = pulled(hidden1[...], cotangent[...], collected(1, plan1))
     hop_out[1] = grad1.astype(BF16)
     hop_copy(1).start()
-    each(back_copy, 2, "start", ALL)
+    each(back_copy, 2, "start", NEAR)
+    each(back_copy, 2, "start", ((4, 8),))
     hop_copy(1).wait_recv()
     pack(3, plan0, hop_in[1])
     each(dispatch_copy, 3, "start", ALL)
+    arrived(3, 1)
+    send_back(3, 1, derive(0, 1), True)
+    arrived(3, 0)
+    each(back_copy, 2, "start", ((0, 4),))
+    send_back(3, 0, derive(0, 0), True)
     final[...] = (hidden1[...].astype(F32) + collected(2, plan1)).astype(BF16)
-    arrived(3)
-    derive(0)
-    send_back(3, contract, True)
     grads[...] = pulled(tokens[...], hop_in[1], collected(3, plan0)).astype(BF16)
 
     for ex in range(4):
@@ -315,15 +322,14 @@
     toks, width = tokens.shape[1:]
     hid = w_gate.shape[3]
     lanes = width + 3 * LANES
-    rows = NB * (ROWS + 1)
+    rows = HALF * (ROWS + 2)
     dma = pltpu.SemaphoreType.DMA
     vmem = pl.BlockSpec(memory_space=pltpu.VMEM)
-    anywhere = pl.BlockSpec(memory_space=pl.ANY)
     out = jax.ShapeDtypeStruct((toks, width), BF16)
     final, grads = pl.pallas_call(
         kernel,
         out_shape=(out, out),
-        in_specs=[vmem] * 2 + [anywhere] * 3 + [vmem] * 3,
+        in_specs=[vmem] * 8,
         out_specs=(vmem, vmem),
         scratch_shapes=[
             pltpu.VMEM((2 * hid, width), BF16),
@@ -333,20 +339,17 @@
             pltpu.VMEM((4, NB * ROWS, lanes), BF16),
             pltpu.VMEM((4, NB * ROWS, lanes), BF16),
             pltpu.VMEM((4, NB * ROWS, lanes), BF16),
-            pltpu.VMEM((3, NB * ROWS, LANES), F32),
-            pltpu.VMEM((rows, width), BF16),
-            pltpu.VMEM((2, rows, 2 * hid), F32),
-            pltpu.VMEM((2, rows, 2 * hid), F32),
+            pltpu.VMEM((3, HALF * ROWS, LANES), F32),
+            pltpu.VMEM((2, rows, width), BF16),
+            pltpu.VMEM((2, 2, rows, 2 * hid), F32),
+            pltpu.VMEM((2, 2, rows, 2 * hid), F32),
             pltpu.VMEM((toks, width), BF16),
             pltpu.VMEM((2, toks, width), BF16),
             pltpu.VMEM((2, toks, width), BF16),
-            pltpu.VMEM((rows, 2 * hid), BF16),
-            pltpu.VMEM((rows, 2 * hid), BF16),
             dma((4, NB)),
             dma((4, NB)),
             dma((4, NB)),
             dma((4, NB)),
-            dma((3,)),
             dma((3,)),
             dma((3,)),
             dma((2,)),

time: 228 us -> 228 us (level)
  the two profiles are of different devices: /device:TPU:312 before, /device:TPU:74 now
where the time goes in v3:
time: 228 us
  Pallas kernels  224 us (98%)
  local copies, waits for them, and re-layouts  2.49 us (1%)
    pallas_call x1, Pallas kernels, local(): pl.pallas_call(kernel, out_shape=(out, out), in_specs=[vmem] * 8, out_spe...  224 us

profile of v3, /device:TPU:74, one launch (start us, length us, event | category | flops | bytes accessed | tf_op | source)
XLA Modules:
  0.0 227.6 jit_solution(17862145160888079614)
XLA Ops:
  0.6 224.4 %shard_map.95 = (bf16[64,2560]{1,0:T(8,128)(2,1)}, bf16[64,2560]{1,0:T(8,128)(2,1)}) custom-call(bf16[64,2560]{1,0:T(8,128)(2,1)} %bitcast.18, f32[1,2560]{1,0:T(1,128)} %gain.1, bf16[192,2560]{1,0:T(8,128)(2,1)} %bitcast.13, bf16[192,2560]{1,0:T(8,128)(2,1)} %bitcast.14, bf16[192,2560]{1,0:T(8,128)(2,1)} %bitcast.15, s32[2,64]{1,0:T(2,128)} %bitcast.20, ...), custom_call_target="tpu_custom_call" | custom-call | tf_op jit(solution)/shard_map/pallas_call | solution.py:329
  225.1 0.0 copy-start
  225.1 1.8 copy.12
  226.8 0.0 copy-done
  226.8 0.7 copy.13
Async XLA Ops:
  225.1 1.8 copy-start

commit v4 on v3

--- a/solution.py
+++ b/solution.py
@@ -18,6 +18,7 @@
 FAR, NEAR = ((0, 8),), ((8, SELF), (SELF + 1, NB))
 ALL = ((0, SELF), (SELF + 1, NB))
 PARTS = (FAR, NEAR)
+LAST, MIDDLE = ((0, 4),), ((4, 8),)
 HALF = 8
 
 
@@ -25,7 +26,7 @@
     tokens, gain, w_gate, w_up, w_down, routes, mix, cotangent, final, grads,
     wg, wu, wd, sends, recvs, back_sends, back_recvs, fold, x_all, gates, uppers, hidden1,
     hop_out, hop_in,
-    send_sems, recv_sems, bsend_sems, brecv_sems, w_send, w_recv, hop_send, hop_recv,
+    send_sems, recv_sems, bsend_sems, brecv_sems, w_local, w_send, w_recv, hop_send, hop_recv,
 ):
     width = tokens.shape[1]
     toks = tokens.shape[0]
@@ -56,6 +57,10 @@
     after = {"section": (section + 1) % sections}
     before = {"section": (section + sections - 1) % sections}
 
+    def weight_local(n):
+        src, dst = ((w_gate, wg), (w_up, wu), (w_down, wd))[n]
+        return pltpu.make_async_copy(src, dst.at[0:hid, :], w_local.at[n])
+
     def weight_copy(n):
         src, dst = ((w_gate, wg), (w_up, wu), (w_down, wd))[n]
         return pltpu.make_async_remote_copy(
@@ -79,15 +84,12 @@
 
     barrier = pltpu.get_barrier_semaphore()
 
-    def greet(place_of):
-        def action(i):
-            xd, zd = place_of(i)
-            pl.semaphore_signal(barrier, inc=1, device_id=at(xd, zd), device_id_type=MESH)
-
-        over(ALL, action)
-
-    greet(target)
-    greet(origin)
+    def greet(i):
+        j = i // 4
+        zd = z + (j - 3 + j // 4) * sign
+        pl.semaphore_signal(barrier, inc=1, device_id=at(x + i % 4, zd), device_id_type=MESH)
+
+    over(((0, SELF), (SELF + 1, NB + 4)), greet)
     for neighbour in (partner, after, before):
         pl.semaphore_signal(barrier, inc=1, device_id=neighbour, device_id_type=MESH)
 
@@ -216,11 +218,13 @@
         if part == 1:
             back_recvs[ex, SELF * ROWS : (SELF + 1) * ROWS, :] = back_sends[ex, SELF * ROWS : (SELF + 1) * ROWS, :]
 
-    def collected(ex, step_plan):
+    def collected(ex, step_plan, then=None):
         _, _, puts, put_spills, weight = step_plan
         total = None
         for part in (1, 0):
             each(back_copy, ex, "recv", PARTS[part])
+            if part == 0 and then is not None:
+                then()
             buffer = back_recvs.at[ex, part_rows(part), :]
             spill = unfold_rows(buffer).astype(BF16)
             term = dot(puts[part], buffer[:, :width]) + dot(put_spills[part], spill)
@@ -231,9 +235,9 @@
         gates[step, part] = dot_t(x_all[part], wg[...])
         uppers[step, part] = dot_t(x_all[part], wu[...])
 
-    def expand(step, part):
+    def activate(step, part):
         gate = gates[step, part]
-        return dot((gate * jax.nn.sigmoid(gate) * uppers[step, part]).astype(BF16), wd[...])
+        return (gate * jax.nn.sigmoid(gate) * uppers[step, part]).astype(BF16)
 
     def derive(step, part):
         d_inner = dot_t(x_all[part], wd[...])
@@ -259,52 +263,58 @@
 
     plan0 = plan(0)
     pack(0, plan0, normed(tokens[...]))
-    pl.semaphore_wait(barrier, 2 * (NB - 1) + 3)
+    pl.semaphore_wait(barrier, NB + 3 + 3)
     weight_copy(0).start()
     weight_copy(1).start()
     each(dispatch_copy, 0, "start", ALL)
     plan1 = plan(1)
     pack(1, plan1, cotangent[...])
     each(dispatch_copy, 1, "start", NEAR)
-    for own, pair in ((w_gate, wg), (w_up, wu), (w_down, wd)):
-        pair[0:hid, :] = own[...]
+    for n in range(3):
+        weight_local(n).start()
     x_all[:, HALF * ROWS + 8 :, :] = jnp.zeros((2, 8, width), BF16)
     arrived(0, 1)
     arrived(0, 0)
     weight_copy(2).start()
+    for n in range(3):
+        weight_local(n).wait()
     weight_copy(0).wait_recv()
     weight_copy(1).wait_recv()
     project(0, 0)
     project(0, 1)
+    far, near = activate(0, 0), activate(0, 1)
     weight_copy(2).wait_recv()
-    send_back(0, 0, expand(0, 0), True)
-    send_back(0, 1, expand(0, 1), True)
-    hop_out[0] = (tokens[...].astype(F32) + collected(0, plan0)).astype(BF16)
+    each(dispatch_copy, 1, "start", MIDDLE)
+    send_back(0, 0, dot(far, wd[...]), True)
+    send_back(0, 1, dot(near, wd[...]), True)
+    combined = collected(0, plan0, lambda: each(dispatch_copy, 1, "start", LAST))
+    hop_out[0] = (tokens[...].astype(F32) + combined).astype(BF16)
     hop_copy(0).start()
-    each(dispatch_copy, 1, "start", FAR)
     hop_copy(0).wait_recv()
     hidden1[...] = hop_in[0]
     pack(2, plan1, normed(hidden1[...]))
     each(dispatch_copy, 2, "start", ALL)
-    for part in (1, 0):
-        arrived(2, part)
-        project(1, part)
-        arrived(1, part)
-        send_back(1, part, derive(1, part), True)
-    send_back(2, 1, expand(1, 1), False)
-    send_back(2, 0, expand(1, 0), False)
-    grad1 = pulled(hidden1[...], cotangent[...], collected(1, plan1))
-    hop_out[1] = grad1.astype(BF16)
+    arrived(2, 1)
+    project(1, 1)
+    arrived(1, 1)
+    send_back(1, 1, derive(1, 1), True)
+    send_back(2, 1, dot(activate(1, 1), wd[...]), False)
+    arrived(2, 0)
+    each(back_copy, 2, "start", NEAR)
+    project(1, 0)
+    arrived(1, 0)
+    send_back(1, 0, derive(1, 0), True)
+    send_back(2, 0, dot(activate(1, 0), wd[...]), False)
+    d_normed = collected(1, plan1, lambda: each(back_copy, 2, "start", LAST))
+    hop_out[1] = pulled(hidden1[...], cotangent[...], d_normed).astype(BF16)
     hop_copy(1).start()
-    each(back_copy, 2, "start", NEAR)
-    each(back_copy, 2, "start", ((4, 8),))
     hop_copy(1).wait_recv()
     pack(3, plan0, hop_in[1])
     each(dispatch_copy, 3, "start", ALL)
     arrived(3, 1)
     send_back(3, 1, derive(0, 1), True)
     arrived(3, 0)
-    each(back_copy, 2, "start", ((0, 4),))
+    each(back_copy, 2, "start", MIDDLE)
     send_back(3, 0, derive(0, 0), True)
     final[...] = (hidden1[...].astype(F32) + collected(2, plan1)).astype(BF16)
     grads[...] = pulled(tokens[...], hop_in[1], collected(3, plan0)).astype(BF16)
@@ -325,11 +335,12 @@
     rows = HALF * (ROWS + 2)
     dma = pltpu.SemaphoreType.DMA
     vmem = pl.BlockSpec(memory_space=pltpu.VMEM)
+    anywhere = pl.BlockSpec(memory_space=pl.ANY)
     out = jax.ShapeDtypeStruct((toks, width), BF16)
     final, grads = pl.pallas_call(
         kernel,
         out_shape=(out, out),
-        in_specs=[vmem] * 8,
+        in_specs=[vmem] * 2 + [anywhere] * 3 + [vmem] * 3,
         out_specs=(vmem, vmem),
         scratch_shapes=[
             pltpu.VMEM((2 * hid, width), BF16),
@@ -352,6 +363,7 @@
             dma((4, NB)),
             dma((3,)),
             dma((3,)),
+            dma((3,)),
             dma((2,)),
             dma((2,)),
         ],

time: 228 us -> 225 us (0.987)
  the two profiles are of different devices: /device:TPU:74 before, /device:TPU:88 now
where the time goes in v4:
time: 225 us; the launch traced here: 224 us
  Pallas kernels  221 us (98%)
  local copies, waits for them, and re-layouts  2.49 us (1%)
    pallas_call x1, Pallas kernels, local(): pl.pallas_call(kernel, out_shape=(out, out), in_specs=[vmem] * 2 + [anywh...  221 us

profile of v4, /device:TPU:88, one launch (start us, length us, event | category | flops | bytes accessed | tf_op | source)
XLA Modules:
  0.0 224.4 jit_solution(5752810388950928585)
XLA Ops:
  0.6 221.3 %shard_map.95 = (bf16[64,2560]{1,0:T(8,128)(2,1)}, bf16[64,2560]{1,0:T(8,128)(2,1)}) custom-call(bf16[64,2560]{1,0:T(8,128)(2,1)} %bitcast.18, f32[1,2560]{1,0:T(1,128)} %gain.1, bf16[192,2560]{1,0:T(8,128)(2,1)} %bitcast.13, bf16[192,2560]{1,0:T(8,128)(2,1)} %bitcast.14, bf16[192,2560]{1,0:T(8,128)(2,1)} %bitcast.15, s32[2,64]{1,0:T(2,128)} %bitcast.20, ...), custom_call_target="tpu_custom_call" | custom-call | tf_op jit(solution)/shard_map/pallas_call | solution.py:340
  221.9 0.0 copy-start
  221.9 1.8 copy.12
  223.7 0.0 copy-done
  223.7 0.7 copy.13
Async XLA Ops:
  221.9 1.8 copy-start

commit v5 on v4

--- a/solution.py
+++ b/solution.py
@@ -68,9 +68,13 @@
             device_id=partner, device_id_type=MESH,
         )
 
-    def hop_copy(n):
+    def hop_rows(h):
+        return slice(h * toks // 2, (h + 1) * toks // 2)
+
+    def hop_copy(n, h):
+        rows = hop_rows(h)
         return pltpu.make_async_remote_copy(
-            src_ref=hop_out.at[n], dst_ref=hop_in.at[n], send_sem=hop_send.at[n], recv_sem=hop_recv.at[n],
+            src_ref=hop_out.at[n, rows, :], dst_ref=hop_in.at[n, rows, :], send_sem=hop_send.at[n, h], recv_sem=hop_recv.at[n, h],
             device_id=after if n == 0 else before, device_id_type=MESH,
         )
 
@@ -218,18 +222,20 @@
         if part == 1:
             back_recvs[ex, SELF * ROWS : (SELF + 1) * ROWS, :] = back_sends[ex, SELF * ROWS : (SELF + 1) * ROWS, :]
 
-    def collected(ex, step_plan, then=None):
+    def collected(ex, step_plan, then, count):
         _, _, puts, put_spills, weight = step_plan
-        total = None
+        total = [0.0] * count
         for part in (1, 0):
             each(back_copy, ex, "recv", PARTS[part])
-            if part == 0 and then is not None:
+            if part == 0:
                 then()
             buffer = back_recvs.at[ex, part_rows(part), :]
             spill = unfold_rows(buffer).astype(BF16)
-            term = dot(puts[part], buffer[:, :width]) + dot(put_spills[part], spill)
-            total = term if total is None else total + term
-        return weight * total
+            for h in range(count):
+                rows = slice(h * toks // count, (h + 1) * toks // count)
+                total[h] += dot(puts[part][rows], buffer[:, :width]) + dot(put_spills[part][rows], spill)
+                if part == 0:
+                    yield rows, weight[rows] * total[h]
 
     def project(step, part):
         gates[step, part] = dot_t(x_all[part], wg[...])
@@ -287,12 +293,14 @@
     each(dispatch_copy, 1, "start", MIDDLE)
     send_back(0, 0, dot(far, wd[...]), True)
     send_back(0, 1, dot(near, wd[...]), True)
-    combined = collected(0, plan0, lambda: each(dispatch_copy, 1, "start", LAST))
-    hop_out[0] = (tokens[...].astype(F32) + combined).astype(BF16)
-    hop_copy(0).start()
-    hop_copy(0).wait_recv()
+    for h, (rows, combined) in enumerate(collected(0, plan0, lambda: each(dispatch_copy, 1, "start", LAST), 2)):
+        hop_out[0, rows, :] = (tokens[rows, :].astype(F32) + combined).astype(BF16)
+        hop_copy(0, h).start()
+    for h in range(2):
+        hop_copy(0, h).wait_recv()
+        hidden1[hop_rows(h), :] = normed(hop_in[0, hop_rows(h), :])
+    pack(2, plan1, hidden1[...])
     hidden1[...] = hop_in[0]
-    pack(2, plan1, normed(hidden1[...]))
     each(dispatch_copy, 2, "start", ALL)
     arrived(2, 1)
     project(1, 1)
@@ -305,10 +313,11 @@
     arrived(1, 0)
     send_back(1, 0, derive(1, 0), True)
     send_back(2, 0, dot(activate(1, 0), wd[...]), False)
-    d_normed = collected(1, plan1, lambda: each(back_copy, 2, "start", LAST))
-    hop_out[1] = pulled(hidden1[...], cotangent[...], d_normed).astype(BF16)
-    hop_copy(1).start()
-    hop_copy(1).wait_recv()
+    for h, (rows, d_normed) in enumerate(collected(1, plan1, lambda: each(back_copy, 2, "start", LAST), 2)):
+        hop_out[1, rows, :] = pulled(hidden1[rows, :], cotangent[rows, :], d_normed).astype(BF16)
+        hop_copy(1, h).start()
+    for h in range(2):
+        hop_copy(1, h).wait_recv()
     pack(3, plan0, hop_in[1])
     each(dispatch_copy, 3, "start", ALL)
     arrived(3, 1)
@@ -316,8 +325,10 @@
     arrived(3, 0)
     each(back_copy, 2, "start", MIDDLE)
     send_back(3, 0, derive(0, 0), True)
-    final[...] = (hidden1[...].astype(F32) + collected(2, plan1)).astype(BF16)
-    grads[...] = pulled(tokens[...], hop_in[1], collected(3, plan0)).astype(BF16)
+    for rows, combined in collected(2, plan1, lambda: None, 1):
+        final[rows, :] = (hidden1[rows, :].astype(F32) + combined).astype(BF16)
+    for rows, d_normed in collected(3, plan0, lambda: None, 1):
+        grads[rows, :] = pulled(tokens[rows, :], hop_in[1, rows, :], d_normed).astype(BF16)
 
     for ex in range(4):
         each(dispatch_copy, ex, "sent", ALL)
@@ -325,7 +336,8 @@
     for n in range(3):
         weight_copy(n).wait_send()
     for n in range(2):
-        hop_copy(n).wait_send()
+        for h in range(2):
+            hop_copy(n, h).wait_send()
 
 
 def local(tokens, norm_gain, w_gate, w_up, w_down, routes, mix_weights, cotangent):
@@ -364,8 +376,8 @@
             dma((3,)),
             dma((3,)),
             dma((3,)),
-            dma((2,)),
-            dma((2,)),
+            dma((2, 2)),
+            dma((2, 2)),
         ],
         compiler_params=pltpu.CompilerParams(
             collective_id=0, has_side_effects=True, vmem_limit_bytes=56 * 1024 * 1024

time: 225 us -> 223 us (level)
  the two profiles are of different devices: /device:TPU:88 before, /device:TPU:24 now
where the time goes in v5:
time: 223 us
  Pallas kernels  220 us (99%)
  local copies, waits for them, and re-layouts  2.49 us (1%)
    pallas_call x1, Pallas kernels, local(): pl.pallas_call(kernel, out_shape=(out, out), in_specs=[vmem] * 2 + [anywh...  220 us

profile of v5, /device:TPU:24, one launch (start us, length us, event | category | flops | bytes accessed | tf_op | source)
XLA Modules:
  0.0 222.8 jit_solution(17528186010675685979)
XLA Ops:
  0.6 219.7 %shard_map.95 = (bf16[64,2560]{1,0:T(8,128)(2,1)}, bf16[64,2560]{1,0:T(8,128)(2,1)}) custom-call(bf16[64,2560]{1,0:T(8,128)(2,1)} %bitcast.18, f32[1,2560]{1,0:T(1,128)} %gain.1, bf16[192,2560]{1,0:T(8,128)(2,1)} %bitcast.13, bf16[192,2560]{1,0:T(8,128)(2,1)} %bitcast.14, bf16[192,2560]{1,0:T(8,128)(2,1)} %bitcast.15, s32[2,64]{1,0:T(2,128)} %bitcast.20, ...), custom_call_target="tpu_custom_call" | custom-call | tf_op jit(solution)/shard_map/pallas_call | solution.py:352
  220.3 0.0 copy-start
  220.3 1.8 copy.12
  222.1 0.0 copy-done
  222.1 0.7 copy.13
Async XLA Ops:
  220.3 1.8 copy-start

commit v6 on v5

--- a/solution.py
+++ b/solution.py
@@ -245,8 +245,10 @@
         gate = gates[step, part]
         return (gate * jax.nn.sigmoid(gate) * uppers[step, part]).astype(BF16)
 
-    def derive(step, part):
-        d_inner = dot_t(x_all[part], wd[...])
+    def pushed(part):
+        return dot_t(x_all[part], wd[...])
+
+    def derive(step, part, d_inner):
         gate = gates[step, part]
         r = jax.nn.sigmoid(gate)
         d_gate = (d_inner * uppers[step, part] * r * (1.0 + gate * (1.0 - r))).astype(BF16)
@@ -260,9 +262,8 @@
         values = hidden.astype(F32)
         return (values * inv_scale(values) * gain[...]).astype(BF16)
 
-    def pulled(hidden, grad, d_normed):
+    def pulled(hidden, r, grad, d_normed):
         values = hidden.astype(F32)
-        r = inv_scale(values)
         scaled = d_normed * gain[...]
         mean = jnp.mean(scaled * values, axis=-1, keepdims=True)
         return grad.astype(F32) + r * scaled - values * (r * r * r * mean)
@@ -302,33 +303,37 @@
     pack(2, plan1, hidden1[...])
     hidden1[...] = hop_in[0]
     each(dispatch_copy, 2, "start", ALL)
+    root1 = inv_scale(hidden1[...].astype(F32))
+    arrived(1, 1)
+    d_near = pushed(1)
     arrived(2, 1)
     project(1, 1)
-    arrived(1, 1)
-    send_back(1, 1, derive(1, 1), True)
+    send_back(1, 1, derive(1, 1, d_near), True)
     send_back(2, 1, dot(activate(1, 1), wd[...]), False)
+    arrived(1, 0)
+    d_far = pushed(0)
     arrived(2, 0)
     each(back_copy, 2, "start", NEAR)
     project(1, 0)
-    arrived(1, 0)
-    send_back(1, 0, derive(1, 0), True)
+    send_back(1, 0, derive(1, 0, d_far), True)
     send_back(2, 0, dot(activate(1, 0), wd[...]), False)
     for h, (rows, d_normed) in enumerate(collected(1, plan1, lambda: each(back_copy, 2, "start", LAST), 2)):
-        hop_out[1, rows, :] = pulled(hidden1[rows, :], cotangent[rows, :], d_normed).astype(BF16)
+        hop_out[1, rows, :] = pulled(hidden1[rows, :], root1[rows], cotangent[rows, :], d_normed).astype(BF16)
         hop_copy(1, h).start()
     for h in range(2):
         hop_copy(1, h).wait_recv()
     pack(3, plan0, hop_in[1])
     each(dispatch_copy, 3, "start", ALL)
     arrived(3, 1)
-    send_back(3, 1, derive(0, 1), True)
+    send_back(3, 1, derive(0, 1, pushed(1)), True)
     arrived(3, 0)
     each(back_copy, 2, "start", MIDDLE)
-    send_back(3, 0, derive(0, 0), True)
+    send_back(3, 0, derive(0, 0, pushed(0)), True)
     for rows, combined in collected(2, plan1, lambda: None, 1):
         final[rows, :] = (hidden1[rows, :].astype(F32) + combined).astype(BF16)
+    root0 = inv_scale(tokens[...].astype(F32))
     for rows, d_normed in collected(3, plan0, lambda: None, 1):
-        grads[rows, :] = pulled(tokens[rows, :], hop_in[1, rows, :], d_normed).astype(BF16)
+        grads[rows, :] = pulled(tokens[rows, :], root0[rows], hop_in[1, rows, :], d_normed).astype(BF16)
 
     for ex in range(4):
         each(dispatch_copy, ex, "sent", ALL)

time: 223 us -> 223 us (level)
  the two profiles are of different devices: /device:TPU:24 before, /device:TPU:88 now
where the time goes in v6:
time: 223 us
  Pallas kernels  220 us (99%)
  local copies, waits for them, and re-layouts  2.49 us (1%)
    pallas_call x1, Pallas kernels, local(): pl.pallas_call(kernel, out_shape=(out, out), in_specs=[vmem] * 2 + [anywh...  220 us

profile of v6, /device:TPU:88, one launch (start us, length us, event | category | flops | bytes accessed | tf_op | source)
XLA Modules:
  0.0 223.3 jit_solution(4924259145702792635)
XLA Ops:
  0.6 220.2 %shard_map.95 = (bf16[64,2560]{1,0:T(8,128)(2,1)}, bf16[64,2560]{1,0:T(8,128)(2,1)}) custom-call(bf16[64,2560]{1,0:T(8,128)(2,1)} %bitcast.18, f32[1,2560]{1,0:T(1,128)} %gain.1, bf16[192,2560]{1,0:T(8,128)(2,1)} %bitcast.13, bf16[192,2560]{1,0:T(8,128)(2,1)} %bitcast.14, bf16[192,2560]{1,0:T(8,128)(2,1)} %bitcast.15, s32[2,64]{1,0:T(2,128)} %bitcast.20, ...), custom_call_target="tpu_custom_call" | custom-call | tf_op jit(solution)/shard_map/pallas_call | solution.py:357
  220.8 0.0 copy-start
  220.8 1.8 copy.12
  222.6 0.0 copy-done
  222.6 0.7 copy.13
Async XLA Ops:
  220.8 1.8 copy-start

commit v7 on v5

--- a/solution.py
+++ b/solution.py
@@ -340,6 +340,17 @@
             hop_copy(n, h).wait_send()
 
 
+def hand_out(final, grads, final_out, grads_out, sems):
+    copies = [
+        pltpu.make_async_copy(final, final_out, sems.at[0]),
+        pltpu.make_async_copy(grads, grads_out, sems.at[1]),
+    ]
+    for copy in copies:
+        copy.start()
+    for copy in copies:
+        copy.wait()
+
+
 def local(tokens, norm_gain, w_gate, w_up, w_down, routes, mix_weights, cotangent):
     toks, width = tokens.shape[1:]
     hid = w_gate.shape[3]
@@ -386,6 +397,13 @@
         tokens[0], norm_gain, w_gate[0, 0].T, w_up[0, 0].T, w_down[0, 0],
         routes[0, :, :, 0], mix_weights[0, :, :, 0], cotangent[0],
     )
+    final, grads = pl.pallas_call(
+        hand_out,
+        out_shape=(out, out),
+        in_specs=[anywhere] * 2,
+        out_specs=(anywhere, anywhere),
+        scratch_shapes=[dma((2,))],
+    )(final, grads)
     return final[None], grads[None]
 
 

time: 223 us -> 241 us (1.081)
  Pallas kernels: 220 us -> 241 us
  local copies, waits for them, and re-layouts: 2.49 us -> 0 us
    pallas_call x0 -> x1, Pallas kernels: none -> 21 us  [local(): pl.pallas_call(hand_out, out_shape=(out, out), in_specs=[anywhere] * 2, o...]
    unnamed x4 -> x0, local copies, waits for them, and re-layouts: 2.49 us -> none
where the time goes in v7:
time: 241 us
  Pallas kernels  241 us (100%)
    pallas_call x1, Pallas kernels, local(): pl.pallas_call(kernel, out_shape=(out, out), in_specs=[vmem] * 2 + [anywh...  220 us
    pallas_call x1, Pallas kernels, local(): pl.pallas_call(hand_out, out_shape=(out, out), in_specs=[anywhere] * 2, o...  21 us

profile of v7, /device:TPU:24, one launch (start us, length us, event | category | flops | bytes accessed | tf_op | source)
XLA Modules:
  0.0 241.3 jit_solution(2203322554606878064)
XLA Ops:
  0.6 219.7 %shard_map.95 = (bf16[64,2560]{1,0:T(8,128)(2,1)}, bf16[64,2560]{1,0:T(8,128)(2,1)}) custom-call(bf16[64,2560]{1,0:T(8,128)(2,1)} %bitcast.16, f32[1,2560]{1,0:T(1,128)} %gain.1, bf16[192,2560]{1,0:T(8,128)(2,1)} %bitcast.13, bf16[192,2560]{1,0:T(8,128)(2,1)} %bitcast.14, bf16[192,2560]{1,0:T(8,128)(2,1)} %bitcast.15, s32[2,64]{1,0:T(2,128)} %bitcast.18, ...), custom_call_target="tpu_custom_call" | custom-call | tf_op jit(solution)/shard_map/pallas_call | solution.py:363
  220.3 21.0 %shard_map.96 = (bf16[64,2560]{1,0:T(8,128)(2,1)}, bf16[64,2560]{1,0:T(8,128)(2,1)}) custom-call(bf16[64,2560]{1,0:T(8,128)(2,1)} %get-tuple-element.6.final, bf16[64,2560]{1,0:T(8,128)(2,1)} %get-tuple-element.7.grads), custom_call_target="tpu_custom_call" | custom-call | tf_op jit(solution)/shard_map/pallas_call | solution.py:400
